TPU v7x, 256 devices: a whole 4x4x8 slice. The times are simulated.
256 devices in a mesh: lat: 8 (over z_lo, core), lon: 8 (over z_hi, x), chan: 4 (over y).
Axes of the slice: x: 4, y: 4, z: 8 (z_hi: 2, z_lo: 4; z = z_hi * 4 + z_lo), core: 2. Of those that a mesh axis runs over, the one named last changes fastest.
Arguments:
- queries: bfloat16 [128, 64, 2560], P('lat', 'lon', 'chan'), may hold values from -8 to 8
- keys: bfloat16 [128, 64, 2560], P('lat', 'lon', 'chan'), may hold values from -8 to 8
- values: bfloat16 [128, 64, 2560], P('lat', 'lon', 'chan'), may hold values from -6 to 6
- attn_out: bfloat16 [128, 64, 2560], P('lat', 'lon', 'chan'), may hold values from -6 to 6
- grad_out: bfloat16 [128, 64, 5120], P('lat', 'lon', 'chan'), may hold values from -6 to 6
- w_out: bfloat16 [5120, 2560], P(('lat', 'lon'), 'chan'), may hold values from -0.078125 to 0.078125
- bias_table: float32 [20, 25, 13], P('chan'), may hold values from -5 to 5
- key_mask: int32 [128, 64], replicated, may hold values 0 or 1
Outputs:
- grad_queries: bfloat16 [128, 64, 2560], P('lat', 'lon', 'chan')
- grad_keys: bfloat16 [128, 64, 2560], P('lat', 'lon', 'chan')
- grad_values: bfloat16 [128, 64, 2560], P('lat', 'lon', 'chan')
- grad_wout: float32 [5120, 2560], P(('lat', 'lon'), 'chan')
- grad_table: float32 [20, 25, 13], P('chan')
All inputs are finite; a program needn't handle non-finite values.
Results may differ from a plain program's by a relative error of at most 0.007.
Values may be sent and summed in bfloat16 or wider, within the bound.
No kernel may reach another device: no remote copies, remote signals or barrier semaphores. Data moves between devices by JAX's collectives and lax.ppermute only.
A program may use at most 128 MiB of HBM per device.

v0:
```python
import jax
import jax.numpy as jnp
from jax import lax
from jax.sharding import PartitionSpec as P

HEAD_DIM = 128
WIN = 13


def extended_2(value, sides, width, wrap):
    for axis, dim in sides:
        count, length = (lax.axis_size(axis), value.shape[dim])
        up = [(i, (i + 1) % count) for i in range(count if wrap else count - 1)]
        down = [(j, i) for i, j in up]
        last = lax.slice_in_dim(value, length - width, length, axis=dim)
        leading = lax.slice_in_dim(value, 0, width, axis=dim)
        before = lax.ppermute(last, axis, up)
        after = lax.ppermute(leading, axis, down)
        value = jnp.concatenate([before, value, after], axis=dim)
    return value


def fold_lon(extended, core_width):
    full_width = extended.shape[2]
    reach_cells = (full_width - core_width) // 2
    rim_cells = jnp.concatenate(
        [extended[:, :, :reach_cells], extended[:, :, full_width - reach_cells :]], axis=2
    )
    received = extended_2(rim_cells.astype(jnp.bfloat16), (("lon", 2),), reach_cells, True).astype(
        rim_cells.dtype
    )
    middle = extended[:, :, reach_cells : full_width - reach_cells]
    front_add = jnp.pad(
        received[:, :, :reach_cells], ((0, 0), (0, 0), (0, core_width - reach_cells), (0, 0))
    )
    back_add = jnp.pad(
        received[:, :, 3 * reach_cells :], ((0, 0), (0, 0), (core_width - reach_cells, 0), (0, 0))
    )
    return middle + front_add + back_add


def fold_lat(extended, core_width):
    full_width = extended.shape[1]
    reach_cells = (full_width - core_width) // 2
    rim_cells = jnp.concatenate(
        [extended[:, :reach_cells], extended[:, full_width - reach_cells :]], axis=1
    )
    received = extended_2(rim_cells.astype(jnp.bfloat16), (("lat", 1),), reach_cells, False).astype(
        rim_cells.dtype
    )
    middle = extended[:, reach_cells : full_width - reach_cells]
    front_add = jnp.pad(
        received[:, :reach_cells], ((0, 0), (0, core_width - reach_cells), (0, 0), (0, 0))
    )
    back_add = jnp.pad(
        received[:, 3 * reach_cells :], ((0, 0), (core_width - reach_cells, 0), (0, 0), (0, 0))
    )
    return middle + front_add + back_add


def local(queries, keys, values, attn_out, grad_out, w_out, bias_table, key_mask):
    lat_rows, lon_cols, chan_width = queries.shape
    head_count = bias_table.shape[0]
    reach_cells = WIN // 2
    score_scale = HEAD_DIM ** (-0.5)
    tokens = lat_rows * lon_cols
    ext_rows = lat_rows + 2 * reach_cells
    ext_cols = lon_cols + 2 * reach_cells
    row_block = 4
    key_span = row_block + WIN - 1
    block_count = lat_rows // row_block
    block_rows = row_block * lon_cols
    block_keys = key_span * ext_cols
    offset_rows = 2 * WIN - 1
    low_pad = row_block - 1
    lat_total = lat_rows * lax.axis_size("lat")
    lon_total = lon_cols * lax.axis_size("lon")
    contract_lead = (((0,), (0,)), ((), ()))
    full_grad = lax.all_gather(grad_out, "chan", axis=2, tiled=True).reshape(tokens, -1)
    grad_cols = jnp.transpose(full_grad)
    slab_part = grad_cols
    grad_attn = lax.dot_general(
        slab_part,
        lax.all_gather(w_out, ("lat", "lon"), axis=0, tiled=True),
        contract_lead,
        preferred_element_type=jnp.float32,
    ).astype(jnp.bfloat16)
    kv_pair = jnp.stack([keys, values])
    extended = extended_2(kv_pair, (("lat", 1), ("lon", 2)), reach_cells, True)
    lat_first = lax.axis_index("lat") * lat_rows
    lon_first = lax.axis_index("lon") * lon_cols
    ext_col = lon_first - reach_cells + jnp.arange(ext_cols, dtype=jnp.int32)
    wrap_col = ext_col % lon_total
    mask_cols = jnp.take(key_mask, wrap_col, axis=1)
    mark_cols = wrap_col % 4 == 0
    rel_lon = (
        jnp.arange(ext_cols, dtype=jnp.int32)[None, :]
        - jnp.arange(lon_cols, dtype=jnp.int32)[:, None]
    )
    in_lon = (rel_lon >= 0) & (rel_lon < WIN)
    lon_pick = jnp.clip(rel_lon, 0, WIN - 1)
    lon_table = jnp.take(bias_table, lon_pick, axis=2).transpose(0, 2, 1, 3)
    table_pad = jnp.pad(lon_table, ((0, 0), (0, 0), (low_pad, low_pad), (0, 0)))
    query_heads = queries.reshape(lat_rows, lon_cols, head_count, HEAD_DIM)
    grad_heads = grad_attn.reshape(lat_rows, lon_cols, head_count, HEAD_DIM)

    def block_step(state_pair, block_index):
        grad_pair, table_acc = state_pair
        local_first = block_index * row_block
        top_row = lat_first + local_first
        key_first = jnp.clip(top_row - reach_cells, 0, lat_total - key_span)
        key_local = key_first - (lat_first - reach_cells)
        query_rows = top_row + jnp.arange(row_block, dtype=jnp.int32)
        window_first = jnp.clip(query_rows - reach_cells, 0, lat_total - WIN)
        key_glob = key_first + jnp.arange(key_span, dtype=jnp.int32)
        in_lat = (key_glob[None, :] >= window_first[:, None]) & (
            key_glob[None, :] < window_first[:, None] + WIN
        )
        mask_rows = lax.dynamic_slice_in_dim(mask_cols, key_first, key_span, 0)
        valid_keys = (mask_rows == 1) | (key_glob % 4 == 0)[:, None] & mark_cols[None, :]
        allowed = in_lat[:, None, :, None] & in_lon[None, :, None, :] & valid_keys[None, None, :, :]
        allowed = allowed.reshape(block_rows, block_keys)
        shifts = key_first - query_rows + (WIN - 1) + low_pad
        bias_parts = [
            lax.dynamic_slice_in_dim(table_pad, shifts[row_pos], key_span, 2)
            for row_pos in range(row_block)
        ]
        bias_rows = jnp.stack(bias_parts, axis=1).reshape(head_count, block_rows, block_keys)
        query_block = lax.dynamic_slice_in_dim(query_heads, local_first, row_block, 0).reshape(
            block_rows, head_count, HEAD_DIM
        )
        grad_block = lax.dynamic_slice_in_dim(grad_heads, local_first, row_block, 0).reshape(
            block_rows, head_count, HEAD_DIM
        )
        pair_block = lax.dynamic_slice_in_dim(extended, key_local, key_span, 1).reshape(
            2, block_keys, head_count, HEAD_DIM
        )
        key_block = pair_block[0]
        value_block = pair_block[1]
        scores = (
            score_scale
            * jnp.einsum("qhd,khd->hqk", query_block, key_block, preferred_element_type=jnp.float32)
            + bias_rows
        )
        scores = jnp.where(allowed[None], scores, -1e30)
        row_max = jnp.max(scores, axis=2, keepdims=True)
        weights_exp = jnp.exp(scores - row_max)
        prob_rows = weights_exp / jnp.sum(weights_exp, axis=2, keepdims=True)
        grad_prob = jnp.einsum(
            "qhd,khd->hqk", grad_block, value_block, preferred_element_type=jnp.float32
        )
        row_delta = jnp.sum(prob_rows * grad_prob, axis=2, keepdims=True)
        dscore = prob_rows * (grad_prob - row_delta)
        score_grid = dscore.reshape(head_count, row_block, lon_cols, key_span, ext_cols)
        score_grid = score_grid.transpose(0, 1, 3, 2, 4).reshape(
            head_count, row_block, key_span, lon_cols * ext_cols
        )
        for row_pos in range(row_block):
            prior_sum = lax.dynamic_slice_in_dim(table_acc, shifts[row_pos], key_span, 1)
            table_acc = lax.dynamic_update_slice_in_dim(
                table_acc, prior_sum + score_grid[:, row_pos], shifts[row_pos], 1
            )
        dscore_low = dscore.astype(jnp.bfloat16)
        prob_low = prob_rows.astype(jnp.bfloat16)
        grad_query = (
            score_scale
            * jnp.einsum("hqk,khd->qhd", dscore_low, key_block, preferred_element_type=jnp.float32)
        ).astype(jnp.bfloat16)
        key_part = score_scale * jnp.einsum(
            "hqk,qhd->khd", dscore_low, query_block, preferred_element_type=jnp.float32
        )
        value_part = jnp.einsum(
            "hqk,qhd->khd", prob_low, grad_block, preferred_element_type=jnp.float32
        )
        new_part = jnp.stack([key_part, value_part]).reshape(2, key_span, ext_cols, chan_width)
        prior_pair = lax.dynamic_slice_in_dim(grad_pair, key_local, key_span, 1)
        grad_pair = lax.dynamic_update_slice_in_dim(grad_pair, prior_pair + new_part, key_local, 1)
        return ((grad_pair, table_acc), grad_query)

    zero_pair = jnp.zeros((2, ext_rows, ext_cols, chan_width), jnp.float32)
    zero_table = jnp.zeros(
        (head_count, offset_rows + 2 * low_pad, lon_cols * ext_cols), jnp.float32
    )
    (grad_pair, table_acc), query_blocks = lax.scan(
        block_step, (zero_pair, zero_table), jnp.arange(block_count, dtype=jnp.int32)
    )
    grad_queries = query_blocks.reshape(lat_rows, lon_cols, chan_width)
    table_core = table_acc[:, low_pad : low_pad + offset_rows].reshape(
        head_count, offset_rows, lon_cols, ext_cols
    )
    col_take = (
        jnp.arange(lon_cols, dtype=jnp.int32)[:, None] + jnp.arange(WIN, dtype=jnp.int32)[None, :]
    )
    col_take = jnp.broadcast_to(
        col_take[None, None, :, :], (head_count, offset_rows, lon_cols, WIN)
    )
    table_local = jnp.sum(jnp.take_along_axis(table_core, col_take, axis=3), axis=2)
    grad_table = lax.psum(table_local, ("lat", "lon"))
    folded = fold_lat(fold_lon(grad_pair, lon_cols), lat_rows)
    grad_keys = folded[0].astype(jnp.bfloat16)
    grad_values = folded[1].astype(jnp.bfloat16)
    saved_out = attn_out.reshape(tokens, chan_width)
    slab_part = grad_cols
    grad_wout = lax.psum_scatter(
        jnp.dot(slab_part, saved_out, preferred_element_type=jnp.float32),
        ("lat", "lon"),
        scatter_dimension=0,
        tiled=True,
    )
    return (grad_queries, grad_keys, grad_values, grad_wout, grad_table)


def solution(mesh):
    return jax.shard_map(
        local,
        mesh=mesh,
        in_specs=(
            P("lat", "lon", "chan"),
            P("lat", "lon", "chan"),
            P("lat", "lon", "chan"),
            P("lat", "lon", "chan"),
            P("lat", "lon", "chan"),
            P(("lat", "lon"), "chan"),
            P("chan", None, None),
            P(),
        ),
        out_specs=(
            P("lat", "lon", "chan"),
            P("lat", "lon", "chan"),
            P("lat", "lon", "chan"),
            P(("lat", "lon"), "chan"),
            P("chan", None, None),
        ),
        check_vma=False,
    )
```

profile of v0, /device:TPU:240, one launch (start us, length us, event | category | flops | bytes accessed | tf_op | source)
XLA Modules:
  0.0 933.4 jit_solution(14924076082434811027)
XLA Ops:
  7.2 1.8 copy.63
  9.8 26.9 %all-gather.3.cloned.1.call-done = bf16[16,8,5120]{2,0,1:T(8,128)(2,1)} async-done(((bf16[16,8,1280]{2,0,1:T(8,128)(2,1)}), bf16[16,8,5120]{2,0,1:T(8,128)(2,1)}) %all-gather.3.cloned.1.call-update) | async-done | bytes 1310736 | tf_op jit(solution)/shard_map/all_gather | solution.py:79
  36.7 7.9 convolution_bitcast_fusion.1
  45.8 1.7 collective-permute-start.1
  51.5 4.6 collective-permute-start.3
  56.1 1.4 gather_fusion.1
  59.1 11.4 %collective-permute-done.3 = bf16[2,28,6,640]{3,0,2,1:T(2,128)(2,1)S(1)} collective-permute-done((bf16[2,28,6,640]{3,0,2,1:T(2,128)(2,1)S(1)}, bf16[2,28,6,640]{3,0,2,1:T(2,128)(2,1)S(1)}, u32[]{:S(2)}, u32[]{:S(2)}) %collective-permute-start.3) | collective-permute-done | bytes 430112 | tf_op jit(solution)/shard_map/ppermute | solution.py:18
  70.6 10.3 %collective-permute-done.2 = bf16[2,28,6,640]{3,0,2,1:T(2,128)(2,1)S(1)} collective-permute-done((bf16[2,28,6,640]{3,0,2,1:T(2,128)(2,1)S(1)}, bf16[2,28,6,640]{3,0,2,1:T(2,128)(2,1)S(1)}, u32[]{:S(2)}, u32[]{:S(2)}) %collective-permute-start.2) | collective-permute-done | bytes 430112 | tf_op jit(solution)/shard_map/ppermute | solution.py:17
  80.9 2.1 pad_maximum_fusion.1
  83.0 156.4 %all-gather.5.cloned.1.call-done = bf16[5120,640]{1,0:T(8,128)(2,1)} async-done(((bf16[80,640]{1,0:T(8,128)(2,1)}), bf16[5120,640]{1,0:T(8,128)(2,1)}) %all-gather.5.cloned.1.call-update) | async-done | bytes 6553616 | tf_op jit(solution)/shard_map/all_gather | solution.py:84
  239.4 4.6 fusion.42
  244.0 1.9 broadcast_in_dim.94
  245.9 117.0 %while.18 = (s32[]{:T(128)}, f32[2,28,20,640]{3,2,1,0:T(8,128)}, f32[5,31,160]{2,1,0:T(8,128)S(1)}, bf16[4,32,5,128]{3,1,2,0:T(8,128)(2,1)}, s32[4]{0:T(128)S(1)...) while((s32[]{:T(128)}, f32[2,28,20,640]{3,2,1,0:T(8,128)}, ...), condition=%wide.region_4.5_spmd.clone, body=%wide.region_0.0_spmd.clone.sunk | while | flops 67648624 | bytes 32509632 | solution.py:184
  257.6 1.3 constant_dynamic-slice_fusion.7
  259.8 1.9 dynamic-slice_bitcast_fusion.5
  272.1 3.0 fusion.106
  286.8 1.3 constant_dynamic-slice_fusion.7
  289.0 1.9 dynamic-slice_bitcast_fusion.5
  301.4 3.0 fusion.106
  316.0 1.3 constant_dynamic-slice_fusion.7
  318.3 1.9 dynamic-slice_bitcast_fusion.5
  330.6 3.1 fusion.106
  345.3 1.3 constant_dynamic-slice_fusion.7
  347.5 1.9 dynamic-slice_bitcast_fusion.5
  359.8 3.1 fusion.106
  363.0 2.2 convert.16
  367.6 2.0 collective-permute-start.4
  371.3 155.3 %gather_fusion.2 = f32[13000]{0:T(1024)S(1)} fusion(f32[5,25,8,20]{3,2,1,0:T(8,128)S(1)} %reshape.333, s32[13000]{0:T(1024)S(1)} %reshape.350), kind=kCustom, calls=%fused_computation.2 | custom fusion | bytes 312000 | tf_op jit(solution)/shard_map/jit(take_along_axis)/gather | solution.py:197
  529.9 2.3 fusion.59
  532.3 2.1 collective-permute-start.6
  534.3 4.4 collective-permute-start.7
  539.0 386.1 %psum.7 = f32[5,25,13]{2,1,0:T(8,128)S(1)} all-reduce(f32[5,25,13]{2,1,0:T(8,128)S(1)} %select_reduce_fusion), channel_id=1, replica_groups=mesh['lat'=8,'lon'=8,'chan'=4] {'lat','lon'}, use_global_device_ids=true, to_apply=%region_7.8 | all-reduce | flops 1625 | bytes 13000 | tf_op jit(solution)/shard_map/psum | solution.py:198
  (297 shorter events, 75.2 us)
Async XLA Ops:
  7.2 29.5 %copy-start = (bf16[16,8,640]{2,1,0:T(8,128)(2,1)S(1)}, bf16[16,8,640]{2,1,0:T(8,128)(2,1)}, u32[]{:S(2)}) copy-start(bf16[16,8,640]{2,1,0:T(8,128)(2,1)} %param.13) | copy-start | bytes 491524
  7.2 29.5 %all-gather.3.cloned.1.call-start = ((), (), s32[]{:S(2)}) async-start(), calls=%async_computation.1 | async-start | bytes 1638400 | tf_op jit(solution)/shard_map/all_gather | solution.py:79
  9.0 230.4 %all-gather.5.cloned.1.call-start = ((), (), s32[]{:S(2)}) async-start(), calls=%async_computation.2 | async-start | bytes 6656000 | tf_op jit(solution)/shard_map/all_gather | solution.py:84
  9.8 917.1 %reduce-scatter.2.cloned.1.call-start = ((), (), s32[]{:S(2)}) async-start(), calls=%async_computation.3 | async-start | bytes 13312000 | tf_op jit(solution)/shard_map/reduce_scatter | solution.py:204
  44.6 3.0 copy-start.8
  45.7 4.4 collective-permute-start
  45.8 4.8 collective-permute-start.1
  50.6 5.5 copy-start.1
  51.5 19.0 %collective-permute-start.3 = (bf16[2,28,6,640]{3,0,2,1:T(2,128)(2,1)S(1)}, bf16[2,28,6,640]{3,0,2,1:T(2,128)(2,1)S(1)}, u32[]{:S(2)}, u32[]{:S(2)}) collective-permute-start(bf16[2,28,6,640]{3,0,2,1:T(2,128)(2,1)S(1)} %copy.59), channel_id=1, source_target_pairs={{4,0},{8,4},{12,8},{16,12},{20,16},{24,20},{28,24},{0,28},{5,1},{9... | collective-permute-start | bytes 1290248 | tf_op jit(solution)/shard_map/ppermute | solution.py:18
  56.1 24.7 %collective-permute-start.2 = (bf16[2,28,6,640]{3,0,2,1:T(2,128)(2,1)S(1)}, bf16[2,28,6,640]{3,0,2,1:T(2,128)(2,1)S(1)}, u32[]{:S(2)}, u32[]{:S(2)}) collective-permute-start(bf16[2,28,6,640]{3,0,2,1:T(2,128)(2,1)S(1)} %copy.58), channel_id=1, source_target_pairs={{0,4},{4,8},{8,12},{12,16},{16,20},{20,24},{24,28},{28,0},{1,5},{5... | collective-permute-start | bytes 1290248 | tf_op jit(solution)/shard_map/ppermute | solution.py:17
  80.9 158.5 %copy-start.11 = (bf16[16,8,5120]{2,0,1:T(8,128)(2,1)S(1)}, bf16[16,8,5120]{2,0,1:T(8,128)(2,1)}, u32[]{:S(2)}) copy-start(bf16[16,8,5120]{2,0,1:T(8,128)(2,1)} %all-gather.3.cloned.1.call-done) | copy-start | bytes 3932164
  245.9 13.4 %copy-start.12 = (bf16[16,8,5,128]{3,1,2,0:T(8,128)(2,1)}, bf16[16,8,5,128]{3,1,2,0:T(8,128)(2,1)S(1)}, u32[]{:S(2)}) copy-start(bf16[16,8,5,128]{3,1,2,0:T(8,128)(2,1)S(1)} %get-tuple-element.541) | copy-start | bytes 491524 | tf_op jit(solution)/shard_map/while
  272.1 3.0 copy-start.13
  275.2 13.4 %copy-start.12 = (bf16[16,8,5,128]{3,1,2,0:T(8,128)(2,1)}, bf16[16,8,5,128]{3,1,2,0:T(8,128)(2,1)S(1)}, u32[]{:S(2)}) copy-start(bf16[16,8,5,128]{3,1,2,0:T(8,128)(2,1)S(1)} %get-tuple-element.541) | copy-start | bytes 491524 | tf_op jit(solution)/shard_map/while
  301.4 3.0 copy-start.13
  304.4 13.4 %copy-start.12 = (bf16[16,8,5,128]{3,1,2,0:T(8,128)(2,1)}, bf16[16,8,5,128]{3,1,2,0:T(8,128)(2,1)S(1)}, u32[]{:S(2)}) copy-start(bf16[16,8,5,128]{3,1,2,0:T(8,128)(2,1)S(1)} %get-tuple-element.541) | copy-start | bytes 491524 | tf_op jit(solution)/shard_map/while
  330.6 3.1 copy-start.13
  333.6 13.4 %copy-start.12 = (bf16[16,8,5,128]{3,1,2,0:T(8,128)(2,1)}, bf16[16,8,5,128]{3,1,2,0:T(8,128)(2,1)S(1)}, u32[]{:S(2)}) copy-start(bf16[16,8,5,128]{3,1,2,0:T(8,128)(2,1)S(1)} %get-tuple-element.541) | copy-start | bytes 491524 | tf_op jit(solution)/shard_map/while
  359.8 3.1 copy-start.13
  365.3 4.3 copy-start.4
  365.3 4.3 copy-start.6
  365.3 4.7 copy-start.14
  367.6 159.4 %collective-permute-start.5 = (bf16[2,28,6,640]{3,0,2,1:T(2,128)(2,1)}, bf16[2,28,6,640]{3,0,2,1:T(2,128)(2,1)}, u32[]{:S(2)}, u32[]{:S(2)}) collective-permute-start(bf16[2,28,6,640]{3,0,2,1:T(2,128)(2,1)} %copy.71), channel_id=1, source_target_pairs={{4,0},{8,4},{12,8},{16,12},{20,16},{24,20},{28,24},{0,28},{5,1},{9... | collective-permute-start | bytes 1290248 | tf_op jit(solution)/shard_map/ppermute | solution.py:18
  367.6 160.5 %collective-permute-start.4 = (bf16[2,28,6,640]{3,0,2,1:T(2,128)(2,1)}, bf16[2,28,6,640]{3,0,2,1:T(2,128)(2,1)}, u32[]{:S(2)}, u32[]{:S(2)}) collective-permute-start(bf16[2,28,6,640]{3,0,2,1:T(2,128)(2,1)} %copy.70), channel_id=1, source_target_pairs={{0,4},{4,8},{8,12},{12,16},{16,20},{20,24},{24,28},{28,0},{1,5},{5... | collective-permute-start | bytes 1290248 | tf_op jit(solution)/shard_map/ppermute | solution.py:17
  526.6 2.6 copy-start.5
  526.6 2.6 copy-start.7
  529.9 8.9 copy-start.16
  529.9 8.9 copy-start.18
  529.9 8.9 copy-start.20
  532.2 393.8 %copy-start.22 = (pred[16]{0:T(512)(128)(4,1)S(1)}, pred[16]{0:T(512)(128)(4,1)}, u32[]{:S(2)}) copy-start(pred[16]{0:T(512)(128)(4,1)} %constant.227.clone.1) | copy-start | bytes 52
  532.3 393.6 %collective-permute-start.6 = (bf16[2,6,8,640]{3,2,1,0:T(8,128)(2,1)S(1)}, bf16[2,6,8,640]{3,2,1,0:T(8,128)(2,1)S(1)}, u32[]{:S(2)}, u32[]{:S(2)}) collective-permute-start(bf16[2,6,8,640]{3,2,1,0:T(8,128)(2,1)S(1)} %get-tuple-element.361), channel_id=1, source_target_pairs={{0,32},{32,64},{64,96},{96,128},{128,160},{160,192},{192,224},{1,3... | collective-permute-start | bytes 368648 | tf_op jit(solution)/shard_map/ppermute | solution.py:17
  534.3 391.5 %collective-permute-start.7 = (bf16[2,6,8,640]{3,2,1,0:T(8,128)(2,1)S(1)}, bf16[2,6,8,640]{3,2,1,0:T(8,128)(2,1)S(1)}, u32[]{:S(2)}, u32[]{:S(2)}) collective-permute-start(bf16[2,6,8,640]{3,2,1,0:T(8,128)(2,1)S(1)} %get-tuple-element.362), channel_id=1, source_target_pairs={{32,0},{64,32},{96,64},{128,96},{160,128},{192,160},{224,192},{33,... | collective-permute-start | bytes 368648 | tf_op jit(solution)/shard_map/ppermute | solution.py:18
  (14 other events, 18.8 us)
Sparse Core Ops, SparseCore 0:
  9.8 26.8 all-gather.2
  38.5 200.8 all-gather.4
  242.6 461.3 reduce-scatter.1
where the time goes:
time: 935 us; the launch traced here: 933 us
  blocking collectives  386 us (41%)
  local copies, waits for them, and re-layouts  227 us (24%)
  waiting for transfers between devices  207 us (22%)
  loops' own time  33.7 us (4%)
  other arithmetic  28.7 us (3%)
  matrix products  21.7 us (2%)
  starting transfers between devices  15.1 us (2%)
  between operations  14.2 us (2%)
    psum x1, blocking collectives, local(): grad_table = lax.psum(table_local, ('lat', 'lon'))  386 us
    all_gather x1, waiting for transfers between devices, local(): lax.all_gather(w_out, ('lat', 'lon'), axis=0, tiled=True)  156 us
    gather x3, local copies, waits for them, and re-layouts, local(): jnp.take_along_axis(table_core, col_take, axis=3)  156 us
    another operation x1, loops' own time, local(): lax.scan(block_step, (zero_pair, zero_table), jnp.arange(block_count, dty...  33.7 us
    all_gather x1, waiting for transfers between devices, local(): lax.all_gather(grad_out, 'chan', axis=2, tiled=True).reshape(tokens, -1)  26.9 us
  transfers between devices with their start and end apart: 11, of which 6 were waited for; matrix products, arithmetic and copies ran while one was open for 29% of the time, Pallas kernels for 0%

commit v1 on v0

--- a/solution.py
+++ b/solution.py
@@ -5,6 +5,10 @@
 
 HEAD_DIM = 128
 WIN = 13
+
+
+def report_stocks_by_axis(content):
+    return lax.psum(lax.psum(content, "lon"), "lat")
 
 
 def extended_2(value, sides, width, wrap):
@@ -195,7 +199,7 @@
         col_take[None, None, :, :], (head_count, offset_rows, lon_cols, WIN)
     )
     table_local = jnp.sum(jnp.take_along_axis(table_core, col_take, axis=3), axis=2)
-    grad_table = lax.psum(table_local, ("lat", "lon"))
+    grad_table = report_stocks_by_axis(table_local)
     folded = fold_lat(fold_lon(grad_pair, lon_cols), lat_rows)
     grad_keys = folded[0].astype(jnp.bfloat16)
     grad_values = folded[1].astype(jnp.bfloat16)

time: 935 us -> 723 us (0.77)
  blocking collectives: 386 us -> 89.5 us
  waiting for transfers between devices: 207 us -> 287 us
    psum x1 -> x2, blocking collectives: 386 us -> 89.5 us  [report_stocks_by_axis(): return lax.psum(lax.psum(content, 'lon'), 'lat')]
    reduce_scatter x1, waiting for transfers between devices: 0.01 us -> 78.8 us  [local(): lax.psum_scatter(jnp.dot(slab_part, saved_out, preferred_element_type=jnp...]
  transfers between devices with their start and end apart: 11 -> 11, of which waited for: 6 -> 7; matrix products, arithmetic and copies ran while one was open for 29% -> 38% of each run, Pallas kernels for 0% -> 0%
where the time goes in v1:
time: 723 us; the launch traced here: 716 us
  waiting for transfers between devices  287 us (40%)
  local copies, waits for them, and re-layouts  227 us (31%)
  blocking collectives  89.5 us (12%)
  loops' own time  33.9 us (5%)
  other arithmetic  28.8 us (4%)
  matrix products  21.7 us (3%)
  starting transfers between devices  14.2 us (2%)
  between operations  14.2 us (2%)
    all_gather x1, waiting for transfers between devices, local(): lax.all_gather(w_out, ('lat', 'lon'), axis=0, tiled=True)  157 us
    gather x3, local copies, waits for them, and re-layouts, local(): jnp.take_along_axis(table_core, col_take, axis=3)  156 us
    psum x2, blocking collectives, report_stocks_by_axis(): return lax.psum(lax.psum(content, 'lon'), 'lat')  89.5 us
    reduce_scatter x1, waiting for transfers between devices, local(): lax.psum_scatter(jnp.dot(slab_part, saved_out, preferred_element_type=jnp...  78.8 us
    another operation x1, loops' own time, local(): lax.scan(block_step, (zero_pair, zero_table), jnp.arange(block_count, dty...  33.9 us
    all_gather x1, waiting for transfers between devices, local(): lax.all_gather(grad_out, 'chan', axis=2, tiled=True).reshape(tokens, -1)  26.9 us
  transfers between devices with their start and end apart: 11, of which 7 were waited for; matrix products, arithmetic and copies ran while one was open for 38% of the time, Pallas kernels for 0%

profile of v1, /device:TPU:240, one launch (start us, length us, event | category | flops | bytes accessed | tf_op | source)
XLA Modules:
  0.0 716.0 jit_solution(15265825217043670548)
XLA Ops:
  7.2 1.8 copy.63
  9.8 26.9 %all-gather.3.cloned.1.call-done = bf16[16,8,5120]{2,0,1:T(8,128)(2,1)} async-done(((bf16[16,8,1280]{2,0,1:T(8,128)(2,1)}), bf16[16,8,5120]{2,0,1:T(8,128)(2,1)}) %all-gather.3.cloned.1.call-update) | async-done | bytes 1310736 | tf_op jit(solution)/shard_map/all_gather | solution.py:83
  36.7 7.9 %convolution_bitcast_fusion.1 = f32[5120,640]{1,0:T(8,128)} fusion(bf16[16,8,5120]{2,0,1:T(8,128)(2,1)} %all-gather.3.cloned.1.call-done, bf16[16,8,640]{2,1,0:T(8,128)(2,1)S(1)} %copy-done), kind=kOutput, calls=%fused_computation.77 | convolution fusion | flops 838860800 | bytes 14581760 | tf_op jit(solution)/shard_map/dot_general | solution.py:209
  45.8 1.7 collective-permute-start.1
  51.5 4.6 collective-permute-start.3
  56.2 1.4 gather_fusion.1
  59.1 11.3 %collective-permute-done.3 = bf16[2,28,6,640]{3,0,2,1:T(2,128)(2,1)S(1)} collective-permute-done((bf16[2,28,6,640]{3,0,2,1:T(2,128)(2,1)S(1)}, bf16[2,28,6,640]{3,0,2,1:T(2,128)(2,1)S(1)}, u32[]{:S(2)}, u32[]{:S(2)}) %collective-permute-start.3) | collective-permute-done | bytes 430112 | tf_op jit(solution)/shard_map/ppermute | solution.py:22
  70.5 10.5 %collective-permute-done.2 = bf16[2,28,6,640]{3,0,2,1:T(2,128)(2,1)S(1)} collective-permute-done((bf16[2,28,6,640]{3,0,2,1:T(2,128)(2,1)S(1)}, bf16[2,28,6,640]{3,0,2,1:T(2,128)(2,1)S(1)}, u32[]{:S(2)}, u32[]{:S(2)}) %collective-permute-start.2) | collective-permute-done | bytes 430112 | tf_op jit(solution)/shard_map/ppermute | solution.py:21
  81.0 2.1 pad_maximum_fusion.1
  83.1 157.3 %all-gather.5.cloned.1.call-done = bf16[5120,640]{1,0:T(8,128)(2,1)} async-done(((bf16[80,640]{1,0:T(8,128)(2,1)}), bf16[5120,640]{1,0:T(8,128)(2,1)}) %all-gather.5.cloned.1.call-update) | async-done | bytes 6553616 | tf_op jit(solution)/shard_map/all_gather | solution.py:88
  240.4 4.6 fusion.42
  245.0 1.9 broadcast_in_dim.94
  246.9 117.3 %while.18 = (s32[]{:T(128)}, f32[2,28,20,640]{3,2,1,0:T(8,128)}, f32[5,31,160]{2,1,0:T(8,128)S(1)}, bf16[4,32,5,128]{3,1,2,0:T(8,128)(2,1)}, s32[4]{0:T(128)S(1)...) while((s32[]{:T(128)}, f32[2,28,20,640]{3,2,1,0:T(8,128)}, ...), condition=%wide.region_4.5_spmd.clone, body=%wide.region_0.0_spmd.clone.sunk | while | flops 67648624 | bytes 32509632 | solution.py:188
  258.6 1.3 constant_dynamic-slice_fusion.7
  260.8 1.9 dynamic-slice_bitcast_fusion.5
  273.2 3.1 fusion.106
  290.1 1.9 dynamic-slice_bitcast_fusion.5
  302.5 3.1 fusion.106
  319.4 1.9 dynamic-slice_bitcast_fusion.5
  331.7 3.1 fusion.106
  346.5 1.3 constant_dynamic-slice_fusion.7
  348.7 1.9 dynamic-slice_bitcast_fusion.5
  361.1 3.1 fusion.106
  364.2 2.2 convert.16
  368.8 2.0 collective-permute-start.4
  372.5 155.3 %gather_fusion.2 = f32[13000]{0:T(1024)S(1)} fusion(f32[5,25,8,20]{3,2,1,0:T(8,128)S(1)} %reshape.333, s32[13000]{0:T(1024)S(1)} %reshape.350), kind=kCustom, calls=%fused_computation.2 | custom fusion | bytes 312000 | tf_op jit(solution)/shard_map/jit(take_along_axis)/gather | solution.py:201
  531.1 2.4 fusion.59
  533.5 1.9 collective-permute-start.6
  535.4 3.7 collective-permute-start.7
  539.3 55.0 %psum.14 = f32[5,25,13]{2,1,0:T(8,128)S(1)} all-reduce(f32[5,25,13]{2,1,0:T(8,128)S(1)} %select_reduce_fusion), channel_id=1, replica_groups=mesh['lat'=8,'lon'=8,'chan'=4] {'lon'}, use_global_device_ids=true, to_apply=%region_7.8 | all-reduce | flops 1625 | bytes 13000 | tf_op jit(solution)/shard_map/psum | solution.py:11
  594.3 34.5 %psum.15 = f32[5,25,13]{2,1,0:T(8,128)S(1)} all-reduce(f32[5,25,13]{2,1,0:T(8,128)S(1)} %psum.14), channel_id=1, replica_groups=mesh['lat'=8,'lon'=8,'chan'=4] {'lat'}, use_global_device_ids=true, to_apply=%region_8.9 | all-reduce | flops 1625 | bytes 13000 | tf_op jit(solution)/shard_map/psum | solution.py:11
  630.6 78.8 %reduce-scatter.2.cloned.1.call-done = f32[80,640]{1,0:T(8,128)} async-done(((f32[5120,640]{1,0:T(8,128)}), f32[80,640]{1,0:T(8,128)}) %reduce-scatter.2.cloned.1.call-update) | async-done | bytes 204816 | tf_op jit(solution)/shard_map/reduce_scatter | solution.py:208
  (298 shorter events, 77.7 us)
Async XLA Ops:
  7.2 29.5 %copy-start = (bf16[16,8,640]{2,1,0:T(8,128)(2,1)S(1)}, bf16[16,8,640]{2,1,0:T(8,128)(2,1)}, u32[]{:S(2)}) copy-start(bf16[16,8,640]{2,1,0:T(8,128)(2,1)} %param.13) | copy-start | bytes 491524
  7.2 29.5 %all-gather.3.cloned.1.call-start = ((), (), s32[]{:S(2)}) async-start(), calls=%async_computation.1 | async-start | bytes 1638400 | tf_op jit(solution)/shard_map/all_gather | solution.py:83
  9.0 231.4 %all-gather.5.cloned.1.call-start = ((), (), s32[]{:S(2)}) async-start(), calls=%async_computation.2 | async-start | bytes 6656000 | tf_op jit(solution)/shard_map/all_gather | solution.py:88
  9.8 699.7 %reduce-scatter.2.cloned.1.call-start = ((), (), s32[]{:S(2)}) async-start(), calls=%async_computation.3 | async-start | bytes 13312000 | tf_op jit(solution)/shard_map/reduce_scatter | solution.py:208
  44.7 3.0 copy-start.8
  45.7 4.4 collective-permute-start
  45.8 4.8 collective-permute-start.1
  50.6 5.5 copy-start.1
  51.5 18.9 %collective-permute-start.3 = (bf16[2,28,6,640]{3,0,2,1:T(2,128)(2,1)S(1)}, bf16[2,28,6,640]{3,0,2,1:T(2,128)(2,1)S(1)}, u32[]{:S(2)}, u32[]{:S(2)}) collective-permute-start(bf16[2,28,6,640]{3,0,2,1:T(2,128)(2,1)S(1)} %copy.59), channel_id=1, source_target_pairs={{4,0},{8,4},{12,8},{16,12},{20,16},{24,20},{28,24},{0,28},{5,1},{9... | collective-permute-start | bytes 1290248 | tf_op jit(solution)/shard_map/ppermute | solution.py:22
  56.1 24.8 %collective-permute-start.2 = (bf16[2,28,6,640]{3,0,2,1:T(2,128)(2,1)S(1)}, bf16[2,28,6,640]{3,0,2,1:T(2,128)(2,1)S(1)}, u32[]{:S(2)}, u32[]{:S(2)}) collective-permute-start(bf16[2,28,6,640]{3,0,2,1:T(2,128)(2,1)S(1)} %copy.58), channel_id=1, source_target_pairs={{0,4},{4,8},{8,12},{12,16},{16,20},{20,24},{24,28},{28,0},{1,5},{5... | collective-permute-start | bytes 1290248 | tf_op jit(solution)/shard_map/ppermute | solution.py:21
  81.0 159.4 %copy-start.11 = (bf16[16,8,5120]{2,0,1:T(8,128)(2,1)S(1)}, bf16[16,8,5120]{2,0,1:T(8,128)(2,1)}, u32[]{:S(2)}) copy-start(bf16[16,8,5120]{2,0,1:T(8,128)(2,1)} %all-gather.3.cloned.1.call-done) | copy-start | bytes 3932164
  246.9 13.4 %copy-start.12 = (bf16[16,8,5,128]{3,1,2,0:T(8,128)(2,1)}, bf16[16,8,5,128]{3,1,2,0:T(8,128)(2,1)S(1)}, u32[]{:S(2)}) copy-start(bf16[16,8,5,128]{3,1,2,0:T(8,128)(2,1)S(1)} %get-tuple-element.541) | copy-start | bytes 491524 | tf_op jit(solution)/shard_map/while
  273.2 3.1 copy-start.13
  276.2 13.4 %copy-start.12 = (bf16[16,8,5,128]{3,1,2,0:T(8,128)(2,1)}, bf16[16,8,5,128]{3,1,2,0:T(8,128)(2,1)S(1)}, u32[]{:S(2)}) copy-start(bf16[16,8,5,128]{3,1,2,0:T(8,128)(2,1)S(1)} %get-tuple-element.541) | copy-start | bytes 491524 | tf_op jit(solution)/shard_map/while
  302.4 3.1 copy-start.13
  305.5 13.4 %copy-start.12 = (bf16[16,8,5,128]{3,1,2,0:T(8,128)(2,1)}, bf16[16,8,5,128]{3,1,2,0:T(8,128)(2,1)S(1)}, u32[]{:S(2)}) copy-start(bf16[16,8,5,128]{3,1,2,0:T(8,128)(2,1)S(1)} %get-tuple-element.541) | copy-start | bytes 491524 | tf_op jit(solution)/shard_map/while
  331.7 3.1 copy-start.13
  334.8 13.4 %copy-start.12 = (bf16[16,8,5,128]{3,1,2,0:T(8,128)(2,1)}, bf16[16,8,5,128]{3,1,2,0:T(8,128)(2,1)S(1)}, u32[]{:S(2)}) copy-start(bf16[16,8,5,128]{3,1,2,0:T(8,128)(2,1)S(1)} %get-tuple-element.541) | copy-start | bytes 491524 | tf_op jit(solution)/shard_map/while
  361.1 3.1 copy-start.13
  366.5 4.3 copy-start.4
  366.5 4.3 copy-start.6
  366.5 4.7 copy-start.14
  368.8 159.4 %collective-permute-start.5 = (bf16[2,28,6,640]{3,0,2,1:T(2,128)(2,1)}, bf16[2,28,6,640]{3,0,2,1:T(2,128)(2,1)}, u32[]{:S(2)}, u32[]{:S(2)}) collective-permute-start(bf16[2,28,6,640]{3,0,2,1:T(2,128)(2,1)} %copy.71), channel_id=1, source_target_pairs={{4,0},{8,4},{12,8},{16,12},{20,16},{24,20},{28,24},{0,28},{5,1},{9... | collective-permute-start | bytes 1290248 | tf_op jit(solution)/shard_map/ppermute | solution.py:22
  368.8 160.5 %collective-permute-start.4 = (bf16[2,28,6,640]{3,0,2,1:T(2,128)(2,1)}, bf16[2,28,6,640]{3,0,2,1:T(2,128)(2,1)}, u32[]{:S(2)}, u32[]{:S(2)}) collective-permute-start(bf16[2,28,6,640]{3,0,2,1:T(2,128)(2,1)} %copy.70), channel_id=1, source_target_pairs={{0,4},{4,8},{8,12},{12,16},{16,20},{20,24},{24,28},{28,0},{1,5},{5... | collective-permute-start | bytes 1290248 | tf_op jit(solution)/shard_map/ppermute | solution.py:21
  527.8 2.6 copy-start.5
  527.8 2.6 copy-start.7
  531.1 8.0 %copy-start.16 = (s32[8,13]{1,0:T(8,128)S(1)}, s32[8,13]{1,0:T(8,128)}, u32[]{:S(2)}) copy-start(s32[8,13]{1,0:T(8,128)} %copy-done.15) | copy-start | bytes 1252
  531.1 8.0 %copy-start.18 = (s32[8,13]{1,0:T(8,128)S(1)}, s32[8,13]{1,0:T(8,128)}, u32[]{:S(2)}) copy-start(s32[8,13]{1,0:T(8,128)} %copy-done.17) | copy-start | bytes 1252
  531.1 8.1 %copy-start.20 = (pred[8,13]{1,0:T(8,128)(4,1)S(1)}, pred[8,13]{1,0:T(8,128)(4,1)}, u32[]{:S(2)}) copy-start(pred[8,13]{1,0:T(8,128)(4,1)} %copy-done.19) | copy-start | bytes 316
  533.5 96.2 %copy-start.22 = (pred[16]{0:T(512)(128)(4,1)S(1)}, pred[16]{0:T(512)(128)(4,1)}, u32[]{:S(2)}) copy-start(pred[16]{0:T(512)(128)(4,1)} %constant.227.clone.1) | copy-start | bytes 52
  533.5 96.1 %collective-permute-start.6 = (bf16[2,6,8,640]{3,2,1,0:T(8,128)(2,1)S(1)}, bf16[2,6,8,640]{3,2,1,0:T(8,128)(2,1)S(1)}, u32[]{:S(2)}, u32[]{:S(2)}) collective-permute-start(bf16[2,6,8,640]{3,2,1,0:T(8,128)(2,1)S(1)} %get-tuple-element.361), channel_id=1, source_target_pairs={{0,32},{32,64},{64,96},{96,128},{128,160},{160,192},{192,224},{1,3... | collective-permute-start | bytes 368648 | tf_op jit(solution)/shard_map/ppermute | solution.py:21
  535.4 94.2 %collective-permute-start.7 = (bf16[2,6,8,640]{3,2,1,0:T(8,128)(2,1)S(1)}, bf16[2,6,8,640]{3,2,1,0:T(8,128)(2,1)S(1)}, u32[]{:S(2)}, u32[]{:S(2)}) collective-permute-start(bf16[2,6,8,640]{3,2,1,0:T(8,128)(2,1)S(1)} %get-tuple-element.362), channel_id=1, source_target_pairs={{32,0},{64,32},{96,64},{128,96},{160,128},{192,160},{224,192},{33,... | collective-permute-start | bytes 368648 | tf_op jit(solution)/shard_map/ppermute | solution.py:22
  (14 other events, 18.8 us)
Sparse Core Ops, SparseCore 0:
  9.8 26.8 all-gather.2
  38.5 201.8 all-gather.4
  243.5 465.8 reduce-scatter.1
